TPU v7x, 32 devices: a whole 2x2x4 slice. The times are simulated.
32 devices in a mesh: px: 8 (over z, y), py: 4 (over x, core).
Axes of the slice: x: 2, y: 2, z: 4, core: 2. Of those that a mesh axis runs over, the one named last changes fastest.
Arguments:
- spectrum: float32 [2, 1536, 24576], P(None, 'px', 'py'), may hold values from -6 to 6
- concentration: float32 [3072, 24576], P('px', 'py'), may hold values from -6 to 6
- factor_y: float32 [1536, 128], P('py'), may hold values from -0.15625 to 0.15625
- factor_x: float32 [3072, 256], P('px'), may hold values from -0.109375 to 0.109375
Outputs:
- y_compressed: float32 [16, 3072, 128], P('py', 'px')
- core_tensor: float32 [16, 256, 128], P('py', 'px')
All inputs are finite; a program needn't handle non-finite values.
Results may differ from a plain program's by a relative error of at most 0.000076.
Values sent between devices are 32-bit elements; how exact they have to be, the bound alone decides.
No kernel may reach another device: no remote copies, remote signals or barrier semaphores. Data moves between devices by JAX's collectives and lax.ppermute only.
A program may use at most 128 MiB of HBM per device.

v0:
```python
import math
import jax
import jax.numpy as jnp
from jax import lax
from jax.sharding import PartitionSpec as P

NX = 3072
NZ = 16
KX = 1536


def synth_table(first_x, block_width):
    wave = lax.broadcasted_iota(jnp.int32, (KX, block_width), 0)
    column = first_x + lax.broadcasted_iota(jnp.int32, (KX, block_width), 1)
    phase = wave * column % NX
    angle = phase.astype(jnp.float32) * (2.0 * math.pi / NX)
    weight = jnp.where(wave == 0, 1.0, 2.0) / math.sqrt(KX)
    return jnp.concatenate([weight * jnp.cos(angle), -weight * jnp.sin(angle)], axis=0)


def body(spectrum, concentration, factor_y, factor_x):
    x_local = concentration.shape[0]
    line_total = concentration.shape[1]
    y_local = line_total // NZ
    pencil_modes = lax.all_to_all(spectrum, "px", split_axis=2, concat_axis=1, tiled=True)
    line_count = pencil_modes.shape[2]
    stacked_modes = pencil_modes.reshape(2 * KX, line_count)
    block_width = 512
    block_total = NX // block_width

    def fill_block(block_index, velocity):
        first_x = block_index * block_width
        rows = lax.dot_general(
            synth_table(first_x, block_width),
            stacked_modes,
            (((0,), (0,)), ((), ())),
            precision=lax.Precision.HIGHEST,
            preferred_element_type=jnp.float32,
        )
        return lax.dynamic_update_slice_in_dim(velocity, rows, first_x, 0)

    velocity = lax.fori_loop(0, block_total, fill_block, jnp.zeros((NX, line_count), jnp.float32))
    returned = lax.all_to_all(velocity, "px", split_axis=0, concat_axis=1, tiled=True)
    flux_tile = returned * concentration
    flux_cube = flux_tile.reshape(x_local, y_local, NZ)
    rows = flux_cube
    y_compressed = lax.psum_scatter(
        jnp.einsum("xyz,yr->zxr", rows, factor_y, precision=lax.Precision.HIGHEST),
        "py",
        scatter_dimension=0,
        tiled=True,
    )
    core_terms = jnp.einsum("xs,zxr->zsr", factor_x, y_compressed, precision=lax.Precision.HIGHEST)
    core_tensor = lax.psum_scatter(core_terms, "px", scatter_dimension=1, tiled=True)
    return (y_compressed, core_tensor)


def solution(mesh):
    placed = (P(None, "px", "py"), P("px", "py"), P("py", None), P("px", None))
    return jax.shard_map(
        body,
        mesh=mesh,
        in_specs=placed,
        out_specs=(P("py", "px", None), P("py", "px", None)),
        check_vma=False,
    )
```

profile of v0, /device:TPU:0, one launch (start us, length us, event | category | flops | bytes accessed | tf_op | source)
XLA Modules:
  0.0 983.5 jit_solution(7462423224211802599)
XLA Ops:
  7.2 18.4 %copy.17 = f32[2,192,6144]{1,0,2:T(2,128)} copy(f32[2,192,6144]{2,1,0:T(8,128)} %param.6) | data formatting | bytes 18874368 | tf_op args[0]
  25.6 7.3 all-to-all-start
  32.9 273.1 %all-to-all-done = f32[2,192,6144]{1,0,2:T(2,128)} async-done(((f32[2,192,6144]{1,0,2:T(2,128)}), f32[2,192,6144]{1,0,2:T(2,128)}, u32[]{:S(2)}, u32[]{:S(2)}) %all-to-all-start) | async-done | bytes 9437216 | tf_op jit(solution)/shard_map/all_to_all | solution.py:25
  306.0 18.3 %copy.18 = f32[2,8,192,768]{3,2,1,0:T(8,128)} copy(f32[2,8,192,768]{2,0,3,1:T(2,128)} %bitcast.1) | data formatting | bytes 18874368 | tf_op jit(solution)/shard_map/all_to_all | solution.py:25
  324.3 4.2 broadcast_in_dim.15
  328.5 281.5 %while.15 = (s32[]{:T(128)}, f32[3072,768]{1,0:T(8,128)}, f32[3072,768]{1,0:T(8,128)}, s32[]{:T(128)}, s32[]{:T(128)}, /*index=5*/s32[]{:T(128)}, s32[]{:T(128)}) while((s32[]{:T(128)}, f32[3072,768]{1,0:T(8,128)}, f32[3072,768]{1,0:T(8,128)}, s32[]{:T(128)}, s32[]{:T(128)}, /*index=5*/s32[]{:T(128)}, s32[]{:T(128)}) %tuple.56), condition=%wide.region_1.2_spmd, body=%wide.region_0.1_spmd.sunk | while | flops 14505745408 | bytes 23621764 | solution.py:42
  328.5 13.5 %cosine_multiply_fusion.2 = (f32[1536,512]{1,0:T(8,128)S(1)}, f32[1536,512]{1,0:T(8,128)S(1)}) fusion(s32[512]{0:T(512)S(1)} %iota_add_fusion.2, f32[1536]{0:T(1024)S(1)} %get-tuple-element.131, f32[1536]{0:T(1024)S(1)} %get-tuple-element.132), kind=kLoop, calls=%fused_computation.8.clone.1 | loop fusion | flops 8650752 | bytes 6305792 | tf_op jit(solution)/shard_map/while/body/eval_jaxpr/mul | solution.py:18
  342.1 33.4 %fusion.28 = f32[3072,768]{1,0:T(8,128)} fusion(f32[3072,768]{1,0:T(8,128)} %get-tuple-element.143, s32[]{:T(128)S(6)} %select_n.61, f32[3072,768]{1,0:T(8,128)} %get-tuple-element.151, f32[1536,512]{1,0:T(8,128)S(1)} %get-tuple-element.133, f32[1536,512]{1,0:T(8,128)S(1)} %get-tuple-element.134), kind=kOutput, calls=%fused_computation.13.clone.1 | convolution fusion | flops 14497087488 | bytes 17301508 | tf_op jit(solution)/shard_map/while/body/eval_jaxpr/dot_general | solution.py:33
  375.4 13.5 %cosine_multiply_fusion.2 = (f32[1536,512]{1,0:T(8,128)S(1)}, f32[1536,512]{1,0:T(8,128)S(1)}) fusion(s32[512]{0:T(512)S(1)} %iota_add_fusion.2, f32[1536]{0:T(1024)S(1)} %get-tuple-element.131, f32[1536]{0:T(1024)S(1)} %get-tuple-element.132), kind=kLoop, calls=%fused_computation.8.clone.1 | loop fusion | flops 8650752 | bytes 6305792 | tf_op jit(solution)/shard_map/while/body/eval_jaxpr/mul | solution.py:18
  388.9 33.4 %fusion.28 = f32[3072,768]{1,0:T(8,128)} fusion(f32[3072,768]{1,0:T(8,128)} %get-tuple-element.143, s32[]{:T(128)S(6)} %select_n.61, f32[3072,768]{1,0:T(8,128)} %get-tuple-element.151, f32[1536,512]{1,0:T(8,128)S(1)} %get-tuple-element.133, f32[1536,512]{1,0:T(8,128)S(1)} %get-tuple-element.134), kind=kOutput, calls=%fused_computation.13.clone.1 | convolution fusion | flops 14497087488 | bytes 17301508 | tf_op jit(solution)/shard_map/while/body/eval_jaxpr/dot_general | solution.py:33
  422.4 13.5 %cosine_multiply_fusion.2 = (f32[1536,512]{1,0:T(8,128)S(1)}, f32[1536,512]{1,0:T(8,128)S(1)}) fusion(s32[512]{0:T(512)S(1)} %iota_add_fusion.2, f32[1536]{0:T(1024)S(1)} %get-tuple-element.131, f32[1536]{0:T(1024)S(1)} %get-tuple-element.132), kind=kLoop, calls=%fused_computation.8.clone.1 | loop fusion | flops 8650752 | bytes 6305792 | tf_op jit(solution)/shard_map/while/body/eval_jaxpr/mul | solution.py:18
  435.9 33.4 %fusion.28 = f32[3072,768]{1,0:T(8,128)} fusion(f32[3072,768]{1,0:T(8,128)} %get-tuple-element.143, s32[]{:T(128)S(6)} %select_n.61, f32[3072,768]{1,0:T(8,128)} %get-tuple-element.151, f32[1536,512]{1,0:T(8,128)S(1)} %get-tuple-element.133, f32[1536,512]{1,0:T(8,128)S(1)} %get-tuple-element.134), kind=kOutput, calls=%fused_computation.13.clone.1 | convolution fusion | flops 14497087488 | bytes 17301508 | tf_op jit(solution)/shard_map/while/body/eval_jaxpr/dot_general | solution.py:33
  469.3 13.5 %cosine_multiply_fusion.2 = (f32[1536,512]{1,0:T(8,128)S(1)}, f32[1536,512]{1,0:T(8,128)S(1)}) fusion(s32[512]{0:T(512)S(1)} %iota_add_fusion.2, f32[1536]{0:T(1024)S(1)} %get-tuple-element.131, f32[1536]{0:T(1024)S(1)} %get-tuple-element.132), kind=kLoop, calls=%fused_computation.8.clone.1 | loop fusion | flops 8650752 | bytes 6305792 | tf_op jit(solution)/shard_map/while/body/eval_jaxpr/mul | solution.py:18
  482.8 33.4 %fusion.28 = f32[3072,768]{1,0:T(8,128)} fusion(f32[3072,768]{1,0:T(8,128)} %get-tuple-element.143, s32[]{:T(128)S(6)} %select_n.61, f32[3072,768]{1,0:T(8,128)} %get-tuple-element.151, f32[1536,512]{1,0:T(8,128)S(1)} %get-tuple-element.133, f32[1536,512]{1,0:T(8,128)S(1)} %get-tuple-element.134), kind=kOutput, calls=%fused_computation.13.clone.1 | convolution fusion | flops 14497087488 | bytes 17301508 | tf_op jit(solution)/shard_map/while/body/eval_jaxpr/dot_general | solution.py:33
  516.2 13.5 %cosine_multiply_fusion.2 = (f32[1536,512]{1,0:T(8,128)S(1)}, f32[1536,512]{1,0:T(8,128)S(1)}) fusion(s32[512]{0:T(512)S(1)} %iota_add_fusion.2, f32[1536]{0:T(1024)S(1)} %get-tuple-element.131, f32[1536]{0:T(1024)S(1)} %get-tuple-element.132), kind=kLoop, calls=%fused_computation.8.clone.1 | loop fusion | flops 8650752 | bytes 6305792 | tf_op jit(solution)/shard_map/while/body/eval_jaxpr/mul | solution.py:18
  529.7 33.4 %fusion.28 = f32[3072,768]{1,0:T(8,128)} fusion(f32[3072,768]{1,0:T(8,128)} %get-tuple-element.143, s32[]{:T(128)S(6)} %select_n.61, f32[3072,768]{1,0:T(8,128)} %get-tuple-element.151, f32[1536,512]{1,0:T(8,128)S(1)} %get-tuple-element.133, f32[1536,512]{1,0:T(8,128)S(1)} %get-tuple-element.134), kind=kOutput, calls=%fused_computation.13.clone.1 | convolution fusion | flops 14497087488 | bytes 17301508 | tf_op jit(solution)/shard_map/while/body/eval_jaxpr/dot_general | solution.py:33
  563.1 13.5 %cosine_multiply_fusion.2 = (f32[1536,512]{1,0:T(8,128)S(1)}, f32[1536,512]{1,0:T(8,128)S(1)}) fusion(s32[512]{0:T(512)S(1)} %iota_add_fusion.2, f32[1536]{0:T(1024)S(1)} %get-tuple-element.131, f32[1536]{0:T(1024)S(1)} %get-tuple-element.132), kind=kLoop, calls=%fused_computation.8.clone.1 | loop fusion | flops 8650752 | bytes 6305792 | tf_op jit(solution)/shard_map/while/body/eval_jaxpr/mul | solution.py:18
  576.6 33.4 %fusion.28 = f32[3072,768]{1,0:T(8,128)} fusion(f32[3072,768]{1,0:T(8,128)} %get-tuple-element.143, s32[]{:T(128)S(6)} %select_n.61, f32[3072,768]{1,0:T(8,128)} %get-tuple-element.151, f32[1536,512]{1,0:T(8,128)S(1)} %get-tuple-element.133, f32[1536,512]{1,0:T(8,128)S(1)} %get-tuple-element.134), kind=kOutput, calls=%fused_computation.13.clone.1 | convolution fusion | flops 14497087488 | bytes 17301508 | tf_op jit(solution)/shard_map/while/body/eval_jaxpr/dot_general | solution.py:33
  610.1 9.5 copy.19
  619.6 5.0 all-to-all-start.1
  624.7 0.0 reduce-scatter.2.cloned.1.call-start
  624.7 9.6 copy.20
  634.4 195.0 %all-to-all-done.1 = f32[8,384,768]{1,2,0:T(8,128)} async-done(((f32[8,384,768]{1,2,0:T(8,128)}), f32[8,384,768]{1,2,0:T(8,128)}, u32[]{:S(2)}, u32[]{:S(2)}) %all-to-all-start.1) | async-done | bytes 9437216 | tf_op jit(solution)/shard_map/all_to_all | solution.py:43
  829.4 11.2 %bitcast_multiply_fusion = f32[384,6144]{0,1:T(8,128)} fusion(f32[384,6144]{0,1:T(8,128)} %copy.20, f32[8,384,768]{1,2,0:T(8,128)} %all-to-all-done.1), kind=kLoop, calls=%fused_computation.19 | loop fusion | flops 2359296 | bytes 28311552 | tf_op jit(solution)/shard_map/mul | solution.py:44
  840.6 21.0 %fusion.16 = f32[16,384,128]{2,1,0:T(8,128)} fusion(f32[384,384,16]{0,2,1:T(8,128)} %bitcast.26, f32[384,128]{1,0:T(8,128)S(1)} %copy-done.1), kind=kOutput, calls=%fused_computation.22 | convolution fusion | flops 3623878656 | bytes 12779520 | tf_op jit(solution)/shard_map/xyz,yr->zxr/dot_general | solution.py:48
  861.7 37.0 %reduce-scatter.2.cloned.1.call-done = f32[4,384,128]{2,1,0:T(8,128)} async-done(((f32[16,384,128]{2,1,0:T(8,128)}), f32[4,384,128]{2,1,0:T(8,128)}) %reduce-scatter.2.cloned.1.call-update) | async-done | bytes 786448 | tf_op jit(solution)/shard_map/reduce_scatter | solution.py:47
  898.8 2.6 convolution_bitcast_fusion
  901.3 1.0 copy.23
  902.3 0.6 dynamic-slice
  903.6 71.6 %all-reduce.3.cloned.1.call-done = f32[4,256,128]{2,0,1:T(4,128)} async-done(((f32[4,256,128]{2,0,1:T(4,128)}), f32[4,256,128]{2,0,1:T(4,128)}) %all-reduce.3.cloned.1.call-update) | async-done | bytes 524304
  975.2 0.8 constant_dynamic-slice_fusion
  976.1 0.6 copy.24
  (21 shorter events, 0.1 us)
Async XLA Ops:
  7.2 891.6 %copy-start = (f32[384,256]{1,0:T(8,128)S(1)}, f32[384,256]{1,0:T(8,128)}, u32[]{:S(2)}) copy-start(f32[384,256]{1,0:T(8,128)} %param.9) | copy-start | bytes 1179652
  25.6 280.4 %all-to-all-start = ((f32[2,192,6144]{1,0,2:T(2,128)}), f32[2,192,6144]{1,0,2:T(2,128)}, u32[]{:S(2)}, u32[]{:S(2)}) async-start(f32[2,192,6144]{1,0,2:T(2,128)} %copy.17), calls=%async_computation | async-start | bytes 25165824 | tf_op jit(solution)/shard_map/all_to_all | solution.py:25
  619.6 209.8 %all-to-all-start.1 = ((f32[8,384,768]{1,2,0:T(8,128)}), f32[8,384,768]{1,2,0:T(8,128)}, u32[]{:S(2)}, u32[]{:S(2)}) async-start(f32[8,384,768]{1,2,0:T(8,128)} %copy.19), calls=%async_computation.1 | async-start | bytes 18874368 | tf_op jit(solution)/shard_map/all_to_all | solution.py:43
  624.7 274.1 %reduce-scatter.2.cloned.1.call-start = ((), (), s32[]{:S(2)}) async-start(), calls=%async_computation.3 | async-start | bytes 3932160 | tf_op jit(solution)/shard_map/reduce_scatter | solution.py:47
  634.4 206.3 %copy-start.1 = (f32[384,128]{1,0:T(8,128)S(1)}, f32[384,128]{1,0:T(8,128)}, u32[]{:S(2)}) copy-start(f32[384,128]{1,0:T(8,128)} %param.8) | copy-start | bytes 589828
  861.6 40.7 %copy-start.2 = (u32[32]{0:T(128)S(1)}, u32[32]{0:T(128)}, u32[]{:S(2)}) copy-start(u32[32]{0:T(128)} %constant.99) | copy-start | bytes 388
  861.7 113.6 %all-reduce.3.cloned.1.call-start = ((), (), s32[]{:S(2)}) async-start(), calls=%async_computation.4 | async-start | bytes 1048576
Sparse Core Ops, SparseCore 0:
  861.8 36.9 reduce-scatter.1
  902.5 72.7 all-reduce.2
where the time goes:
time: 985 us; the launch traced here: 984 us
  waiting for transfers between devices  577 us (59%)
  matrix products  224 us (23%)
  other arithmetic  92.3 us (9%)
  local copies, waits for them, and re-layouts  63.2 us (6%)
  between operations  14.7 us (1%)
  starting transfers between devices  12.4 us (1%)
    all_to_all x1, waiting for transfers between devices, body(): lax.all_to_all(spectrum, 'px', split_axis=2, concat_axis=1, tiled=True)  273 us
    dot_general x6, matrix products, fill_block(): lax.dot_general(synth_table(first_x, block_width), stacked_modes, (((0,),...  200 us
    all_to_all x1, waiting for transfers between devices, body(): lax.all_to_all(velocity, 'px', split_axis=0, concat_axis=1, tiled=True)  195 us
    mul x6, other arithmetic, synth_table(): weight * jnp.cos(angle)  81 us
    unnamed x3, waiting for transfers between devices  71.7 us
    reduce_scatter x1, waiting for transfers between devices, body(): lax.psum_scatter(jnp.einsum('xyz,yr->zxr', rows, factor_y, precision=lax....  37 us
    unnamed x11, local copies, waits for them, and re-layouts  30.1 us
    dot_general x1, matrix products, body(): jnp.einsum('xyz,yr->zxr', rows, factor_y, precision=lax.Precision.HIGHEST)  21 us
  transfers between devices with their start and end apart: 4, of which 4 were waited for; matrix products, arithmetic and copies ran while one was open for 1% of the time, Pallas kernels for 0%

commit v1 on v0

--- a/solution.py
+++ b/solution.py
@@ -7,6 +7,22 @@
 NX = 3072
 NZ = 16
 KX = 1536
+
+
+def swapped_with_each(shard, axis, split, join):
+    ways, here = (lax.axis_size(axis), lax.axis_index(axis))
+    width = shard.shape[split] // ways
+    shape = list(shard.shape)
+    shape[split] = width
+    height = shape[join]
+    shape[join] = height * ways
+    full = jnp.zeros(shape, shard.dtype)
+    for mask in range(ways):
+        part = lax.dynamic_slice_in_dim(shard, (here ^ mask) * width, width, axis=split)
+        if mask:
+            part = lax.ppermute(part, axis, [(d, d ^ mask) for d in range(ways)])
+        full = lax.dynamic_update_slice_in_dim(full, part, (here ^ mask) * height, axis=join)
+    return full
 
 
 def synth_table(first_x, block_width):
@@ -22,7 +38,7 @@
     x_local = concentration.shape[0]
     line_total = concentration.shape[1]
     y_local = line_total // NZ
-    pencil_modes = lax.all_to_all(spectrum, "px", split_axis=2, concat_axis=1, tiled=True)
+    pencil_modes = swapped_with_each(spectrum, "px", 2, 1)
     line_count = pencil_modes.shape[2]
     stacked_modes = pencil_modes.reshape(2 * KX, line_count)
     block_width = 512

time: 985 us -> 889 us (0.903)
  waiting for transfers between devices: 577 us -> 443 us
  starting transfers between devices: 12.4 us -> 61.1 us
  local copies, waits for them, and re-layouts: 63.2 us -> 53.1 us
    all_to_all x1 -> x0, waiting for transfers between devices: 273 us -> none  [body(): lax.all_to_all(spectrum, 'px', split_axis=2, concat_axis=1, tiled=True)]
    ppermute x0 -> x7, waiting for transfers between devices: none -> 140 us  [swapped_with_each(): part = lax.ppermute(part, axis, [(d, d ^ mask) for d in range(ways)])]
    all_to_all x1, starting transfers between devices: 5.04 us -> 47.6 us  [body(): lax.all_to_all(velocity, 'px', split_axis=0, concat_axis=1, tiled=True)]
    all_to_all x1 -> x0, local copies, waits for them, and re-layouts: 18.3 us -> none  [body(): lax.all_to_all(spectrum, 'px', split_axis=2, concat_axis=1, tiled=True)]
    unnamed x11 -> x18, local copies, waits for them, and re-layouts: 30.1 us -> 14.5 us
    dynamic_update_slice x0 -> x7, local copies, waits for them, and re-layouts: none -> 15.5 us  [swapped_with_each(): lax.dynamic_update_slice_in_dim(full, part, (here ^ mask) * height, axis=...]
    ppermute x0 -> x7, starting transfers between devices: none -> 13.4 us  [swapped_with_each(): part = lax.ppermute(part, axis, [(d, d ^ mask) for d in range(ways)])]
  transfers between devices with their start and end apart: 4 -> 10, of which waited for: 4 -> 7; matrix products, arithmetic and copies ran while one was open for 1% -> 3% of each run, Pallas kernels for 0% -> 0%
where the time goes in v1:
time: 889 us; the launch traced here: 888 us
  waiting for transfers between devices  443 us (50%)
  matrix products  224 us (25%)
  other arithmetic  92.3 us (10%)
  starting transfers between devices  61.1 us (7%)
  local copies, waits for them, and re-layouts  53.1 us (6%)
  between operations  14.8 us (2%)
    dot_general x6, matrix products, fill_block(): lax.dot_general(synth_table(first_x, block_width), stacked_modes, (((0,),...  200 us
    all_to_all x1, waiting for transfers between devices, body(): lax.all_to_all(velocity, 'px', split_axis=0, concat_axis=1, tiled=True)  196 us
    ppermute x7, waiting for transfers between devices, swapped_with_each(): part = lax.ppermute(part, axis, [(d, d ^ mask) for d in range(ways)])  140 us
    mul x6, other arithmetic, synth_table(): weight * jnp.cos(angle)  81 us
    unnamed x3, waiting for transfers between devices  71.7 us
    all_to_all x1, starting transfers between devices, body(): lax.all_to_all(velocity, 'px', split_axis=0, concat_axis=1, tiled=True)  47.6 us
    reduce_scatter x1, waiting for transfers between devices, body(): lax.psum_scatter(jnp.einsum('xyz,yr->zxr', rows, factor_y, precision=lax....  35.4 us
    dot_general x1, matrix products, body(): jnp.einsum('xyz,yr->zxr', rows, factor_y, precision=lax.Precision.HIGHEST)  21 us
  transfers between devices with their start and end apart: 10, of which 7 were waited for; matrix products, arithmetic and copies ran while one was open for 3% of the time, Pallas kernels for 0%

profile of v1, /device:TPU:0, one launch (start us, length us, event | category | flops | bytes accessed | tf_op | source)
XLA Modules:
  0.0 888.2 jit_solution(16352437532129284215)
XLA Ops:
  7.2 5.4 broadcast_in_dim.19
  14.4 2.8 constant_dynamic-slice_fusion
  17.2 3.0 collective-permute-start
  21.7 3.0 collective-permute-start.3
  26.1 20.1 %collective-permute-done = f32[2,192,768]{2,1,0:T(8,128)S(1)} collective-permute-done((f32[2,192,768]{2,1,0:T(8,128)S(1)}, f32[2,192,768]{2,1,0:T(8,128)S(1)}, u32[]{:S(2)}, u32[]{:S(2)}) %collective-permute-start) | collective-permute-done | bytes 1179680 | tf_op jit(solution)/shard_map/ppermute | solution.py:23
  46.2 3.8 collective-permute-start.5
  50.0 48.7 %collective-permute-done.1 = f32[2,192,768]{2,1,0:T(8,128)S(1)} collective-permute-done((f32[2,192,768]{2,1,0:T(8,128)S(1)}, f32[2,192,768]{2,1,0:T(8,128)S(1)}, u32[]{:S(2)}, u32[]{:S(2)}) %collective-permute-start.1) | collective-permute-done | bytes 1179680 | tf_op jit(solution)/shard_map/ppermute | solution.py:23
  104.0 17.6 %collective-permute-done.2 = f32[2,192,768]{2,1,0:T(8,128)} collective-permute-done((f32[2,192,768]{2,1,0:T(8,128)}, f32[2,192,768]{2,1,0:T(8,128)}, u32[]{:S(2)}, u32[]{:S(2)}) %collective-permute-start.2) | collective-permute-done | bytes 1179680 | tf_op jit(solution)/shard_map/ppermute | solution.py:23
  126.3 53.3 %collective-permute-done.4 = f32[2,192,768]{2,1,0:T(8,128)} collective-permute-done((f32[2,192,768]{2,1,0:T(8,128)}, f32[2,192,768]{2,1,0:T(8,128)}, u32[]{:S(2)}, u32[]{:S(2)}) %collective-permute-start.4) | collective-permute-done | bytes 1179680 | tf_op jit(solution)/shard_map/ppermute | solution.py:23
  186.8 4.3 broadcast_in_dim.18
  191.1 281.5 %while.15 = (s32[]{:T(128)}, f32[3072,768]{1,0:T(8,128)}, f32[3072,768]{1,0:T(8,128)}, s32[]{:T(128)}, s32[]{:T(128)}, /*index=5*/s32[]{:T(128)}, s32[]{:T(128)}) while((s32[]{:T(128)}, f32[3072,768]{1,0:T(8,128)}, f32[3072,768]{1,0:T(8,128)}, s32[]{:T(128)}, s32[]{:T(128)}, /*index=5*/s32[]{:T(128)}, s32[]{:T(128)}) %tuple.56), condition=%wide.region_1.2_spmd, body=%wide.region_0.1_spmd.sunk | while | flops 14505745408 | bytes 23621764 | solution.py:58
  191.1 13.5 %cosine_multiply_fusion.2 = (f32[1536,512]{1,0:T(8,128)S(1)}, f32[1536,512]{1,0:T(8,128)S(1)}) fusion(s32[512]{0:T(512)S(1)} %iota_add_fusion.2, f32[1536]{0:T(1024)S(1)} %get-tuple-element.139, f32[1536]{0:T(1024)S(1)} %get-tuple-element.140), kind=kLoop, calls=%fused_computation.8.clone.1 | loop fusion | flops 8650752 | bytes 6305792 | tf_op jit(solution)/shard_map/while/body/eval_jaxpr/mul | solution.py:34
  204.7 33.4 %fusion.28 = f32[3072,768]{1,0:T(8,128)} fusion(f32[3072,768]{1,0:T(8,128)} %get-tuple-element.151, s32[]{:T(128)S(6)} %select_n.125, f32[3072,768]{1,0:T(8,128)} %get-tuple-element.159, f32[1536,512]{1,0:T(8,128)S(1)} %get-tuple-element.141, f32[1536,512]{1,0:T(8,128)S(1)} %get-tuple-element.142), kind=kOutput, calls=%fused_computation.13.clone.1 | convolution fusion | flops 14497087488 | bytes 17301508 | tf_op jit(solution)/shard_map/while/body/eval_jaxpr/dot_general | solution.py:49
  238.0 13.5 %cosine_multiply_fusion.2 = (f32[1536,512]{1,0:T(8,128)S(1)}, f32[1536,512]{1,0:T(8,128)S(1)}) fusion(s32[512]{0:T(512)S(1)} %iota_add_fusion.2, f32[1536]{0:T(1024)S(1)} %get-tuple-element.139, f32[1536]{0:T(1024)S(1)} %get-tuple-element.140), kind=kLoop, calls=%fused_computation.8.clone.1 | loop fusion | flops 8650752 | bytes 6305792 | tf_op jit(solution)/shard_map/while/body/eval_jaxpr/mul | solution.py:34
  251.6 33.4 %fusion.28 = f32[3072,768]{1,0:T(8,128)} fusion(f32[3072,768]{1,0:T(8,128)} %get-tuple-element.151, s32[]{:T(128)S(6)} %select_n.125, f32[3072,768]{1,0:T(8,128)} %get-tuple-element.159, f32[1536,512]{1,0:T(8,128)S(1)} %get-tuple-element.141, f32[1536,512]{1,0:T(8,128)S(1)} %get-tuple-element.142), kind=kOutput, calls=%fused_computation.13.clone.1 | convolution fusion | flops 14497087488 | bytes 17301508 | tf_op jit(solution)/shard_map/while/body/eval_jaxpr/dot_general | solution.py:49
  284.9 13.5 %cosine_multiply_fusion.2 = (f32[1536,512]{1,0:T(8,128)S(1)}, f32[1536,512]{1,0:T(8,128)S(1)}) fusion(s32[512]{0:T(512)S(1)} %iota_add_fusion.2, f32[1536]{0:T(1024)S(1)} %get-tuple-element.139, f32[1536]{0:T(1024)S(1)} %get-tuple-element.140), kind=kLoop, calls=%fused_computation.8.clone.1 | loop fusion | flops 8650752 | bytes 6305792 | tf_op jit(solution)/shard_map/while/body/eval_jaxpr/mul | solution.py:34
  298.5 33.4 %fusion.28 = f32[3072,768]{1,0:T(8,128)} fusion(f32[3072,768]{1,0:T(8,128)} %get-tuple-element.151, s32[]{:T(128)S(6)} %select_n.125, f32[3072,768]{1,0:T(8,128)} %get-tuple-element.159, f32[1536,512]{1,0:T(8,128)S(1)} %get-tuple-element.141, f32[1536,512]{1,0:T(8,128)S(1)} %get-tuple-element.142), kind=kOutput, calls=%fused_computation.13.clone.1 | convolution fusion | flops 14497087488 | bytes 17301508 | tf_op jit(solution)/shard_map/while/body/eval_jaxpr/dot_general | solution.py:49
  331.9 13.5 %cosine_multiply_fusion.2 = (f32[1536,512]{1,0:T(8,128)S(1)}, f32[1536,512]{1,0:T(8,128)S(1)}) fusion(s32[512]{0:T(512)S(1)} %iota_add_fusion.2, f32[1536]{0:T(1024)S(1)} %get-tuple-element.139, f32[1536]{0:T(1024)S(1)} %get-tuple-element.140), kind=kLoop, calls=%fused_computation.8.clone.1 | loop fusion | flops 8650752 | bytes 6305792 | tf_op jit(solution)/shard_map/while/body/eval_jaxpr/mul | solution.py:34
  345.4 33.4 %fusion.28 = f32[3072,768]{1,0:T(8,128)} fusion(f32[3072,768]{1,0:T(8,128)} %get-tuple-element.151, s32[]{:T(128)S(6)} %select_n.125, f32[3072,768]{1,0:T(8,128)} %get-tuple-element.159, f32[1536,512]{1,0:T(8,128)S(1)} %get-tuple-element.141, f32[1536,512]{1,0:T(8,128)S(1)} %get-tuple-element.142), kind=kOutput, calls=%fused_computation.13.clone.1 | convolution fusion | flops 14497087488 | bytes 17301508 | tf_op jit(solution)/shard_map/while/body/eval_jaxpr/dot_general | solution.py:49
  378.8 13.5 %cosine_multiply_fusion.2 = (f32[1536,512]{1,0:T(8,128)S(1)}, f32[1536,512]{1,0:T(8,128)S(1)}) fusion(s32[512]{0:T(512)S(1)} %iota_add_fusion.2, f32[1536]{0:T(1024)S(1)} %get-tuple-element.139, f32[1536]{0:T(1024)S(1)} %get-tuple-element.140), kind=kLoop, calls=%fused_computation.8.clone.1 | loop fusion | flops 8650752 | bytes 6305792 | tf_op jit(solution)/shard_map/while/body/eval_jaxpr/mul | solution.py:34
  392.3 33.4 %fusion.28 = f32[3072,768]{1,0:T(8,128)} fusion(f32[3072,768]{1,0:T(8,128)} %get-tuple-element.151, s32[]{:T(128)S(6)} %select_n.125, f32[3072,768]{1,0:T(8,128)} %get-tuple-element.159, f32[1536,512]{1,0:T(8,128)S(1)} %get-tuple-element.141, f32[1536,512]{1,0:T(8,128)S(1)} %get-tuple-element.142), kind=kOutput, calls=%fused_computation.13.clone.1 | convolution fusion | flops 14497087488 | bytes 17301508 | tf_op jit(solution)/shard_map/while/body/eval_jaxpr/dot_general | solution.py:49
  425.7 13.5 %cosine_multiply_fusion.2 = (f32[1536,512]{1,0:T(8,128)S(1)}, f32[1536,512]{1,0:T(8,128)S(1)}) fusion(s32[512]{0:T(512)S(1)} %iota_add_fusion.2, f32[1536]{0:T(1024)S(1)} %get-tuple-element.139, f32[1536]{0:T(1024)S(1)} %get-tuple-element.140), kind=kLoop, calls=%fused_computation.8.clone.1 | loop fusion | flops 8650752 | bytes 6305792 | tf_op jit(solution)/shard_map/while/body/eval_jaxpr/mul | solution.py:34
  439.2 33.4 %fusion.28 = f32[3072,768]{1,0:T(8,128)} fusion(f32[3072,768]{1,0:T(8,128)} %get-tuple-element.151, s32[]{:T(128)S(6)} %select_n.125, f32[3072,768]{1,0:T(8,128)} %get-tuple-element.159, f32[1536,512]{1,0:T(8,128)S(1)} %get-tuple-element.141, f32[1536,512]{1,0:T(8,128)S(1)} %get-tuple-element.142), kind=kOutput, calls=%fused_computation.13.clone.1 | convolution fusion | flops 14497087488 | bytes 17301508 | tf_op jit(solution)/shard_map/while/body/eval_jaxpr/dot_general | solution.py:49
  472.7 9.6 %copy.15 = f32[8,384,768]{1,2,0:T(8,128)} copy(f32[8,384,768]{2,1,0:T(8,128)} %bitcast.23) | data formatting | bytes 18874368 | tf_op jit(solution)/shard_map/all_to_all | solution.py:59
  482.3 47.6 %all-to-all-start = ((f32[8,384,768]{1,2,0:T(8,128)}), f32[8,384,768]{1,2,0:T(8,128)}, u32[]{:S(2)}, u32[]{:S(2)}) async-start(f32[8,384,768]{1,2,0:T(8,128)} %copy.15), calls=%async_computation | async-start | bytes 18874368 | tf_op jit(solution)/shard_map/all_to_all | solution.py:59
  529.9 9.6 %copy.16 = f32[384,6144]{0,1:T(8,128)} copy(f32[384,6144]{1,0:T(8,128)} %param.7) | data formatting | bytes 18874368 | tf_op args[1]
  539.6 195.9 %all-to-all-done = f32[8,384,768]{1,2,0:T(8,128)} async-done(((f32[8,384,768]{1,2,0:T(8,128)}), f32[8,384,768]{1,2,0:T(8,128)}, u32[]{:S(2)}, u32[]{:S(2)}) %all-to-all-start) | async-done | bytes 9437216 | tf_op jit(solution)/shard_map/all_to_all | solution.py:59
  735.5 11.3 %bitcast_multiply_fusion = f32[384,6144]{0,1:T(8,128)} fusion(f32[384,6144]{0,1:T(8,128)} %copy.16, f32[8,384,768]{1,2,0:T(8,128)} %all-to-all-done), kind=kLoop, calls=%fused_computation.19 | loop fusion | flops 2359296 | bytes 28311552 | tf_op jit(solution)/shard_map/mul | solution.py:60
  746.8 21.0 %fusion.16 = f32[16,384,128]{2,1,0:T(8,128)} fusion(f32[384,384,16]{0,2,1:T(8,128)} %bitcast.22, f32[384,128]{1,0:T(8,128)S(1)} %copy-done.5), kind=kOutput, calls=%fused_computation.22 | convolution fusion | flops 3623878656 | bytes 12779520 | tf_op jit(solution)/shard_map/xyz,yr->zxr/dot_general | solution.py:64
  767.9 35.4 %reduce-scatter.2.cloned.1.call-done = f32[4,384,128]{2,1,0:T(8,128)} async-done(((f32[16,384,128]{2,1,0:T(8,128)}), f32[4,384,128]{2,1,0:T(8,128)}) %reduce-scatter.2.cloned.1.call-update) | async-done | bytes 786448 | tf_op jit(solution)/shard_map/reduce_scatter | solution.py:63
  803.3 2.6 convolution_bitcast_fusion
  808.2 71.7 %all-reduce.3.cloned.1.call-done = f32[4,256,128]{2,0,1:T(4,128)} async-done(((f32[4,256,128]{2,0,1:T(4,128)}), f32[4,256,128]{2,0,1:T(4,128)}) %all-reduce.3.cloned.1.call-update) | async-done | bytes 524304
  (48 shorter events, 25.1 us)
Async XLA Ops:
  7.2 796.1 %copy-start = (f32[384,256]{1,0:T(8,128)S(1)}, f32[384,256]{1,0:T(8,128)}, u32[]{:S(2)}) copy-start(f32[384,256]{1,0:T(8,128)} %param.9) | copy-start | bytes 1179652
  7.2 7.1 copy-start.1
  17.2 29.0 %collective-permute-start = (f32[2,192,768]{2,1,0:T(8,128)S(1)}, f32[2,192,768]{2,1,0:T(8,128)S(1)}, u32[]{:S(2)}, u32[]{:S(2)}) collective-permute-start(f32[2,192,768]{2,1,0:T(8,128)S(1)} %get-tuple-element.113), channel_id=1, source_target_pairs={{0,4},{4,0},{8,12},{12,8},{16,20},{20,16},{24,28},{28,24},{1,5},{5... | collective-permute-start | bytes 3538952 | tf_op jit(solution)/shard_map/ppermute | solution.py:23
  20.2 78.4 %collective-permute-start.1 = (f32[2,192,768]{2,1,0:T(8,128)S(1)}, f32[2,192,768]{2,1,0:T(8,128)S(1)}, u32[]{:S(2)}, u32[]{:S(2)}) collective-permute-start(f32[2,192,768]{2,1,0:T(8,128)S(1)} %get-tuple-element.112), channel_id=1, source_target_pairs={{0,8},{4,12},{8,0},{12,4},{16,24},{20,28},{24,16},{28,20},{1,9},{5... | collective-permute-start | bytes 3538952 | tf_op jit(solution)/shard_map/ppermute | solution.py:23
  21.7 99.9 %collective-permute-start.2 = (f32[2,192,768]{2,1,0:T(8,128)}, f32[2,192,768]{2,1,0:T(8,128)}, u32[]{:S(2)}, u32[]{:S(2)}) collective-permute-start(f32[2,192,768]{2,1,0:T(8,128)} %get-tuple-element.111), channel_id=1, source_target_pairs={{0,12},{4,8},{8,4},{12,0},{16,28},{20,24},{24,20},{28,16},{1,13},{... | collective-permute-start | bytes 3538952 | tf_op jit(solution)/shard_map/ppermute | solution.py:23
  21.7 102.2 %collective-permute-start.3 = (f32[2,192,768]{2,1,0:T(8,128)}, f32[2,192,768]{2,1,0:T(8,128)}, u32[]{:S(2)}, u32[]{:S(2)}) collective-permute-start(f32[2,192,768]{2,1,0:T(8,128)} %get-tuple-element.110), channel_id=1, source_target_pairs={{0,16},{4,20},{8,24},{12,28},{16,0},{20,4},{24,8},{28,12},{1,17},{... | collective-permute-start | bytes 3538952 | tf_op jit(solution)/shard_map/ppermute | solution.py:23
  24.7 154.9 %collective-permute-start.4 = (f32[2,192,768]{2,1,0:T(8,128)}, f32[2,192,768]{2,1,0:T(8,128)}, u32[]{:S(2)}, u32[]{:S(2)}) collective-permute-start(f32[2,192,768]{2,1,0:T(8,128)} %get-tuple-element.109), channel_id=1, source_target_pairs={{0,20},{4,16},{8,28},{12,24},{16,4},{20,0},{24,12},{28,8},{1,21},{... | collective-permute-start | bytes 3538952 | tf_op jit(solution)/shard_map/ppermute | solution.py:23
  46.2 52.4 %copy-start.2 = (f32[2,192,768]{2,1,0:T(8,128)}, f32[2,192,768]{2,1,0:T(8,128)S(1)}, u32[]{:S(2)}) copy-start(f32[2,192,768]{2,1,0:T(8,128)S(1)} %collective-permute-done) | copy-start | bytes 3538948
  46.2 135.8 %collective-permute-start.5 = (f32[2,192,768]{2,1,0:T(8,128)S(1)}, f32[2,192,768]{2,1,0:T(8,128)}, u32[]{:S(2)}, u32[]{:S(2)}) collective-permute-start(f32[2,192,768]{2,1,0:T(8,128)S(1)} %get-tuple-element.115), channel_id=1, source_target_pairs={{0,24},{4,28},{8,16},{12,20},{16,8},{20,12},{24,0},{28,4},{1,25},{... | collective-permute-start | bytes 3538952 | tf_op jit(solution)/shard_map/ppermute | solution.py:23
  98.6 1.0 copy-start.3
  99.6 84.8 %collective-permute-start.6 = (f32[2,192,768]{2,1,0:T(8,128)S(1)}, f32[2,192,768]{2,1,0:T(8,128)}, u32[]{:S(2)}, u32[]{:S(2)}) collective-permute-start(f32[2,192,768]{2,1,0:T(8,128)S(1)} %get-tuple-element.108), channel_id=1, source_target_pairs={{0,28},{4,24},{8,20},{12,16},{16,12},{20,8},{24,4},{28,0},{1,29},{... | collective-permute-start | bytes 3538952 | tf_op jit(solution)/shard_map/ppermute | solution.py:23
  100.4 2.5 copy-start.4
  482.3 253.3 %all-to-all-start = ((f32[8,384,768]{1,2,0:T(8,128)}), f32[8,384,768]{1,2,0:T(8,128)}, u32[]{:S(2)}, u32[]{:S(2)}) async-start(f32[8,384,768]{1,2,0:T(8,128)} %copy.15), calls=%async_computation | async-start | bytes 18874368 | tf_op jit(solution)/shard_map/all_to_all | solution.py:59
  529.9 273.4 %reduce-scatter.2.cloned.1.call-start = ((), (), s32[]{:S(2)}) async-start(), calls=%async_computation.2 | async-start | bytes 3932160 | tf_op jit(solution)/shard_map/reduce_scatter | solution.py:63
  539.6 207.2 %copy-start.5 = (f32[384,128]{1,0:T(8,128)S(1)}, f32[384,128]{1,0:T(8,128)}, u32[]{:S(2)}) copy-start(f32[384,128]{1,0:T(8,128)} %param.8) | copy-start | bytes 589828
  767.8 39.1 %copy-start.6 = (u32[32]{0:T(128)S(1)}, u32[32]{0:T(128)}, u32[]{:S(2)}) copy-start(u32[32]{0:T(128)} %constant.128) | copy-start | bytes 388
  767.8 112.0 %all-reduce.3.cloned.1.call-start = ((), (), s32[]{:S(2)}) async-start(), calls=%async_computation.3 | async-start | bytes 1048576
Sparse Core Ops, SparseCore 0:
  768.0 35.2 reduce-scatter.1
  807.0 72.7 all-reduce.2
